TPU v7x, 256 devices: a whole 4x4x8 slice. The times are simulated.
256 devices in a mesh: snp: 16 (over z, core), trait: 16 (over y, x).
Axes of the slice: x: 4, y: 4, z: 8, core: 2. Of those that a mesh axis runs over, the one named last changes fastest.
Arguments:
- ld_band: float32 [8192, 3072], P('snp'), may hold values from -0.109375 to 0.109375
- marginal: float32 [8192, 4096], P('snp', 'trait'), may hold values from -6 to 6
- effects_init: float32 [8192, 4096], P('snp', 'trait'), may hold values from -6 to 6
- factor_in: float32 [4096, 256], P('trait'), may hold values from -0.09375 to 0.09375
- factor_out: float32 [4096, 256], P('trait'), may hold values from -0.375 to 0.375
- ld_width: int32 [64], replicated, may hold values from 512 to 3072, as said below
- ld_starts: int32 [64], replicated, may hold values from 0 to 8191, as said below
Outputs:
- fitted: float32 [8192, 4096], P('snp', 'trait')
Inputs may be any that keep to these rules, and one draw needn't show every extreme that they name: `ld_width`: every value lies in 512 to 3072; the values 3072 and 512 each occur in every draw. ld_starts[0] is 0, the values rise strictly, and the last one is 8191.
All inputs are finite; a program needn't handle non-finite values.
Results may differ from a plain program's by a relative error of at most 0.0003.
Values sent between devices are 32-bit elements; how exact they have to be, the bound alone decides.
A program may use at most 128 MiB of HBM per device.

v0:
```python
import jax
import jax.numpy as jnp
from jax import lax
from jax.sharding import PartitionSpec as P

STEPS = 2
step_size = 0.5
shrinkage = 0.5


def passed_along(block, axis, distance):
    devices = range(lax.axis_size(axis))
    route = [(i - distance, i) for i in devices if i - distance in devices]
    return lax.ppermute(block, axis, route)


def row_reach(ld_width, ld_starts, row_index, total_rows):
    covered = (ld_starts[None, :] <= row_index[:, None]).astype(jnp.int32)
    following = jnp.concatenate(
        [covered[:, 1:], jnp.zeros((covered.shape[0], 1), jnp.int32)], axis=1
    )
    row_width = jnp.sum((covered - following) * ld_width[None, :], axis=1)
    return jnp.minimum(row_width, total_rows - 1 - row_index)


def shear(ld_rows, reach):
    row_count, band_span = ld_rows.shape
    offsets = lax.broadcasted_iota(jnp.int32, ld_rows.shape, 1)
    masked_band = jnp.where(offsets < reach[:, None], ld_rows, jnp.zeros_like(ld_rows))
    padded = jnp.pad(masked_band, ((0, 0), (0, row_count + 1)))
    full_width = band_span + row_count
    flattened = jnp.concatenate([jnp.zeros((1,), ld_rows.dtype), padded.reshape(-1)])
    return flattened[: row_count * full_width].reshape(row_count, full_width)


def body(ld_band, marginal, effects_init, factor_in, factor_out, ld_width, ld_starts):
    row_count = ld_band.shape[0]
    total_rows = row_count * lax.axis_size("snp")
    hop_count = ld_band.shape[1] // row_count
    local_rows = lax.iota(jnp.int32, row_count)
    row_index = lax.axis_index("snp") * row_count + local_rows
    reach = row_reach(ld_width, ld_starts, row_index, total_rows)
    sheared = shear(ld_band, reach)
    effects = effects_init
    for iteration in range(STEPS):
        ahead = []
        for distance in range(1, hop_count + 1):
            ahead.append(passed_along(effects, "snp", -distance))
        window = jnp.concatenate([effects] + ahead, axis=0)
        upper = jnp.dot(
            sheared, window, precision=lax.Precision.HIGHEST, preferred_element_type=jnp.float32
        )
        transposed = lax.dot_general(
            sheared,
            effects,
            (((0,), (0,)), ((), ())),
            precision=lax.Precision.HIGHEST,
            preferred_element_type=jnp.float32,
        )
        pieces = [
            transposed[tile_index * row_count : (tile_index + 1) * row_count]
            for tile_index in range(hop_count + 1)
        ]
        lower = pieces[0]
        for distance in range(1, hop_count + 1):
            lower = lower + passed_along(pieces[distance], "snp", distance)
        partial_scores = jnp.dot(
            effects, factor_in, precision=lax.Precision.HIGHEST, preferred_element_type=jnp.float32
        )
        scores = lax.psum(partial_scores, "trait")
        projected = lax.dot_general(
            scores,
            factor_out,
            (((1,), (1,)), ((), ())),
            precision=lax.Precision.HIGHEST,
            preferred_element_type=jnp.float32,
        )
        gradient = effects + upper + lower - marginal + shrinkage * (effects - projected)
        effects = effects - step_size * gradient
    return effects


def solution(mesh):
    return jax.shard_map(
        body,
        mesh=mesh,
        in_specs=(
            P("snp", None),
            P("snp", "trait"),
            P("snp", "trait"),
            P("trait", None),
            P("trait", None),
            P(),
            P(),
        ),
        out_specs=P("snp", "trait"),
        check_vma=False,
    )
```

profile of v0, /device:TPU:147, one launch (start us, length us, event | category | flops | bytes accessed | tf_op | source)
XLA Modules:
  0.0 505.4 jit_solution(10433905574596033448)
XLA Ops:
  6.5 2.0 collective-permute-start.5
  8.6 1.9 collective-permute-start.4
  10.5 1.9 collective-permute-start.3
  12.5 1.9 collective-permute-start.1
  14.4 2.7 collective-permute-start
  18.6 3.7 fusion
  22.4 3.6 pad.5
  25.9 11.3 %reshape.18 = f32[1835520]{0:T(1024)} reshape(f32[512,3585]{1,0:T(8,128)} %pad.5) | data formatting | bytes 14684160 | tf_op jit(solution)/shard_map/reshape | solution.py:32
  37.2 6.5 %pad_maximum_fusion = f32[1835008]{0:T(1024)} fusion(f32[1835520]{0:T(1024)} %reshape.18, f32[1]{0:T(128)} %constant.3.clone.1), kind=kLoop, calls=%fused_computation | loop fusion | flops 1835008 | bytes 14682116 | tf_op jit(solution)/shard_map/concatenate | solution.py:32
  43.7 8.4 %reshape.19 = f32[512,3584]{1,0:T(8,128)} reshape(f32[1835008]{0:T(1024)} %pad_maximum_fusion) | data formatting | bytes 14680064 | tf_op jit(solution)/shard_map/reshape | solution.py:33
  52.1 14.6 %fusion.25 = f32[3584,256]{1,0:T(8,128)S(1)} fusion(f32[512,3584]{1,0:T(8,128)} %reshape.19, f32[512,256]{1,0:T(8,128)S(1)} %copy-done.3), kind=kOutput, calls=%fused_computation.51 | convolution fusion | flops 5637144576 | bytes 11534336 | tf_op jit(solution)/shard_map/dot_general | solution.py:53
  66.7 1.9 copy-done.1
  69.9 35.2 %collective-permute-done.1 = f32[512,256]{1,0:T(8,128)S(1)} collective-permute-done((f32[512,256]{1,0:T(8,128)}, f32[512,256]{1,0:T(8,128)S(1)}, u32[]{:S(2)}, u32[]{:S(2)}) %collective-permute-start.1) | collective-permute-done | bytes 524320 | tf_op jit(solution)/shard_map/ppermute | solution.py:14
  105.1 5.4 %collective-permute-start.2 = (f32[512,256]{1,0:T(8,128)S(1)}, f32[512,256]{1,0:T(8,128)}, u32[]{:S(2)}, u32[]{:S(2)}) collective-permute-start(f32[512,256]{1,0:T(8,128)S(1)} %copy-done.3), channel_id=1, source_target_pairs={{48,0},{64,16},{80,32},{96,48},{112,64},{128,80},{144,96},{160,112... | collective-permute-start | bytes 1572872 | tf_op jit(solution)/shard_map/ppermute | solution.py:14
  110.5 2.1 collective-permute-done
  112.6 1.9 collective-permute-start.6
  114.5 1.4 fusion.26
  116.8 1.9 constant_dynamic-update-slice_fusion.5
  118.7 2.0 constant_dynamic-update-slice_fusion.4
  120.7 6.3 %collective-permute-done.2 = f32[512,256]{1,0:T(8,128)} collective-permute-done((f32[512,256]{1,0:T(8,128)S(1)}, f32[512,256]{1,0:T(8,128)}, u32[]{:S(2)}, u32[]{:S(2)}) %collective-permute-start.2) | collective-permute-done | bytes 524320 | tf_op jit(solution)/shard_map/ppermute | solution.py:14
  126.9 1.9 collective-permute-start.11
  128.8 1.9 constant_dynamic-update-slice_fusion.3
  130.7 1.9 collective-permute-start.10
  132.7 1.9 collective-permute-start.9
  134.6 1.9 collective-permute-start.8
  136.5 1.9 collective-permute-start.7
  138.5 1.9 constant_dynamic-update-slice_fusion.2
  140.3 1.9 constant_dynamic-update-slice_fusion.1
  142.2 1.9 constant_dynamic-update-slice_fusion
  144.1 64.9 %all-reduce.5.cloned.1.call-done = f32[512,256]{1,0:T(8,128)} async-done(((f32[512,256]{1,0:T(8,128)}), f32[512,256]{1,0:T(8,128)}) %all-reduce.5.cloned.1.call-update) | async-done | bytes 524304 | tf_op jit(solution)/shard_map/psum | solution.py:70
  209.0 1.8 fusion.2
  210.9 11.0 %collective-permute-done.9 = f32[512,256]{1,0:T(8,128)} collective-permute-done((f32[512,256]{1,0:T(8,128)S(1)}, f32[512,256]{1,0:T(8,128)}, u32[]{:S(2)}, u32[]{:S(2)}) %collective-permute-start.9) | collective-permute-done | bytes 524320 | tf_op jit(solution)/shard_map/ppermute | solution.py:14
  221.9 12.4 %collective-permute-done.8 = f32[512,256]{1,0:T(8,128)} collective-permute-done((f32[512,256]{1,0:T(8,128)S(1)}, f32[512,256]{1,0:T(8,128)}, u32[]{:S(2)}, u32[]{:S(2)}) %collective-permute-start.8) | collective-permute-done | bytes 524320 | tf_op jit(solution)/shard_map/ppermute | solution.py:14
  234.3 11.5 %collective-permute-done.7 = f32[512,256]{1,0:T(8,128)} collective-permute-done((f32[512,256]{1,0:T(8,128)S(1)}, f32[512,256]{1,0:T(8,128)}, u32[]{:S(2)}, u32[]{:S(2)}) %collective-permute-start.7) | collective-permute-done | bytes 524320 | tf_op jit(solution)/shard_map/ppermute | solution.py:14
  245.8 11.2 %constant_dynamic-update-slice_fusion.13 = (f32[3584,256]{1,0:T(8,128)}, f32[512,256]{1,0:T(8,128)S(1)}) fusion(f32[512,256]{1,0:T(8,128)S(1)} %copy-done.3, f32[512,256]{1,0:T(8,128)S(1)} %fusion.2, f32[512,256]{1,0:T(8,128)S(1)} %copy-done.4, f32[512,256]{1,0:T(8,128)} %collective-permute-done.11, f32[512,256]{1,0:T(8,128)} %collective-permute-done.10, ...), kind=kOutput, calls=%fused_computation.46 | convolution fusion | flops 5638717440 | bytes 17301504 | tf_op jit(solution)/shard_map/dot_general | solution.py:50
  257.0 1.9 collective-permute-start.17
  258.9 1.9 collective-permute-start.16
  260.8 2.6 collective-permute-start.14
  263.4 1.9 collective-permute-start.13
  265.4 2.5 collective-permute-start.12
  267.9 12.6 %fusion.27 = f32[3584,256]{1,0:T(8,128)S(1)} fusion(f32[512,3584]{1,0:T(8,128)S(1)} %bitcast.17, f32[512,256]{1,0:T(8,128)S(1)} %get-tuple-element.18), kind=kOutput, calls=%fused_computation.53 | convolution fusion | flops 5637144576 | bytes 11534336 | tf_op jit(solution)/shard_map/dot_general | solution.py:53
  280.4 1.9 copy-done.2
  282.4 1.6 fusion.23
  283.9 63.9 %collective-permute-done.13 = f32[512,256]{1,0:T(8,128)S(1)} collective-permute-done((f32[512,256]{1,0:T(8,128)S(1)}, f32[512,256]{1,0:T(8,128)S(1)}, u32[]{:S(2)}, u32[]{:S(2)}) %collective-permute-start.13) | collective-permute-done | bytes 524320 | tf_op jit(solution)/shard_map/ppermute | solution.py:14
  347.9 2.8 collective-permute-start.15
  350.7 3.6 collective-permute-done.12
  355.1 2.6 collective-permute-start.18
  359.1 1.9 constant_dynamic-update-slice_fusion.12
  361.0 1.9 constant_dynamic-update-slice_fusion.11
  362.9 1.9 collective-permute-start.23
  364.8 1.9 constant_dynamic-update-slice_fusion.10
  366.7 1.9 collective-permute-start.22
  368.6 1.9 collective-permute-start.21
  370.6 2.9 collective-permute-done.15
  373.4 1.9 collective-permute-start.20
  375.4 4.9 collective-permute-start.19
  380.2 1.9 constant_dynamic-update-slice_fusion.9
  382.1 1.9 constant_dynamic-update-slice_fusion.8
  384.0 1.9 constant_dynamic-update-slice_fusion.7
  385.9 75.3 %all-reduce.7.cloned.1.call-done = f32[512,256]{1,0:T(8,128)} async-done(((f32[512,256]{1,0:T(8,128)}), f32[512,256]{1,0:T(8,128)}) %all-reduce.7.cloned.1.call-update) | async-done | bytes 524304 | tf_op jit(solution)/shard_map/psum | solution.py:70
  461.2 1.7 fusion.1
  462.8 7.6 %collective-permute-done.20 = f32[512,256]{1,0:T(8,128)} collective-permute-done((f32[512,256]{1,0:T(8,128)S(1)}, f32[512,256]{1,0:T(8,128)}, u32[]{:S(2)}, u32[]{:S(2)}) %collective-permute-start.20) | collective-permute-done | bytes 524320 | tf_op jit(solution)/shard_map/ppermute | solution.py:14
  470.4 16.8 %collective-permute-done.19 = f32[512,256]{1,0:T(8,128)} collective-permute-done((f32[512,256]{1,0:T(8,128)S(1)}, f32[512,256]{1,0:T(8,128)}, u32[]{:S(2)}, u32[]{:S(2)}) %collective-permute-start.19) | collective-permute-done | bytes 524320 | tf_op jit(solution)/shard_map/ppermute | solution.py:14
  487.2 11.1 %fusion.7 = f32[512,256]{1,0:T(8,128)} fusion(f32[512,256]{1,0:T(8,128)S(1)} %get-tuple-element.18, f32[512,256]{1,0:T(8,128)S(1)} %fusion.1, f32[512,256]{1,0:T(8,128)S(1)} %copy-done.4, f32[512,3584]{1,0:T(8,128)} %reshape.19, f32[3584,256]{1,0:T(8,128)} %constant_dynamic-update-slice_fusion.7, f32[512,256]{1,0:T(8,128)} %collective-permute-done.23, ...), kind=kOutput, calls=%fused_computation.12 | convolution fusion | flops 5638717440 | bytes 16777216 | tf_op jit(solution)/shard_map/dot_general | solution.py:50
  (48 shorter events, 6.0 us)
Async XLA Ops:
  6.5 108.0 %copy-start = (f32[256,256]{1,0:T(8,128)S(1)}, f32[256,256]{1,0:T(8,128)}, u32[]{:S(2)}) copy-start(f32[256,256]{1,0:T(8,128)} %param.10) | copy-start | bytes 786436
  6.5 202.5 %all-reduce.5.cloned.1.call-start = ((), (), s32[]{:S(2)}) async-start(), calls=%async_computation | async-start | bytes 1048576 | tf_op jit(solution)/shard_map/psum | solution.py:70
  6.5 124.2 %collective-permute-start.5 = (f32[512,256]{1,0:T(8,128)}, f32[512,256]{1,0:T(8,128)}, u32[]{:S(2)}, u32[]{:S(2)}) collective-permute-start(f32[512,256]{1,0:T(8,128)} %param.9), channel_id=1, source_target_pairs={{96,0},{112,16},{128,32},{144,48},{160,64},{176,80},{192,96},{208,... | collective-permute-start | bytes 1572872 | tf_op jit(solution)/shard_map/ppermute | solution.py:14
  8.6 124.1 %collective-permute-start.4 = (f32[512,256]{1,0:T(8,128)}, f32[512,256]{1,0:T(8,128)}, u32[]{:S(2)}, u32[]{:S(2)}) collective-permute-start(f32[512,256]{1,0:T(8,128)} %param.9), channel_id=1, source_target_pairs={{80,0},{96,16},{112,32},{128,48},{144,64},{160,80},{176,96},{192,1... | collective-permute-start | bytes 1572872 | tf_op jit(solution)/shard_map/ppermute | solution.py:14
  10.5 124.1 %collective-permute-start.3 = (f32[512,256]{1,0:T(8,128)}, f32[512,256]{1,0:T(8,128)}, u32[]{:S(2)}, u32[]{:S(2)}) collective-permute-start(f32[512,256]{1,0:T(8,128)} %param.9), channel_id=1, source_target_pairs={{64,0},{80,16},{96,32},{112,48},{128,64},{144,80},{160,96},{176,11... | collective-permute-start | bytes 1572872 | tf_op jit(solution)/shard_map/ppermute | solution.py:14
  12.5 92.6 %collective-permute-start.1 = (f32[512,256]{1,0:T(8,128)}, f32[512,256]{1,0:T(8,128)S(1)}, u32[]{:S(2)}, u32[]{:S(2)}) collective-permute-start(f32[512,256]{1,0:T(8,128)} %param.9), channel_id=1, source_target_pairs={{32,0},{48,16},{64,32},{80,48},{96,64},{112,80},{128,96},{144,112}... | collective-permute-start | bytes 1572872 | tf_op jit(solution)/shard_map/ppermute | solution.py:14
  14.4 98.2 %collective-permute-start = (f32[512,256]{1,0:T(8,128)}, f32[512,256]{1,0:T(8,128)}, u32[]{:S(2)}, u32[]{:S(2)}) collective-permute-start(f32[512,256]{1,0:T(8,128)} %param.9), channel_id=1, source_target_pairs={{16,0},{32,16},{48,32},{64,48},{80,64},{96,80},{112,96},{128,112},... | collective-permute-start | bytes 1572872 | tf_op jit(solution)/shard_map/ppermute | solution.py:14
  43.7 8.4 %copy-start.3 = (f32[512,256]{1,0:T(8,128)S(1)}, f32[512,256]{1,0:T(8,128)}, u32[]{:S(2)}) copy-start(f32[512,256]{1,0:T(8,128)} %param.9) | copy-start | bytes 1572868
  66.7 1.9 copy-start.1
  105.1 11.7 %copy-start.7 = (f32[512,256]{1,0:T(8,128)}, f32[512,256]{1,0:T(8,128)S(1)}, u32[]{:S(2)}) copy-start(f32[512,256]{1,0:T(8,128)S(1)} %collective-permute-done.1) | copy-start | bytes 1572868
  105.1 21.8 %collective-permute-start.2 = (f32[512,256]{1,0:T(8,128)S(1)}, f32[512,256]{1,0:T(8,128)}, u32[]{:S(2)}, u32[]{:S(2)}) collective-permute-start(f32[512,256]{1,0:T(8,128)S(1)} %copy-done.3), channel_id=1, source_target_pairs={{48,0},{64,16},{80,32},{96,48},{112,64},{128,80},{144,96},{160,112... | collective-permute-start | bytes 1572872 | tf_op jit(solution)/shard_map/ppermute | solution.py:14
  112.6 23.9 %collective-permute-start.6 = (f32[512,256]{1,0:T(8,128)}, f32[512,256]{1,0:T(8,128)}, u32[]{:S(2)}, u32[]{:S(2)}) collective-permute-start(f32[512,256]{1,0:T(8,128)} %get-tuple-element.11), channel_id=1, source_target_pairs={{0,16},{16,32},{32,48},{48,64},{64,80},{80,96},{96,112},{112,128},... | collective-permute-start | bytes 1572872 | tf_op jit(solution)/shard_map/ppermute | solution.py:14
  115.9 93.1 %copy-start.5 = (f32[256,256]{1,0:T(8,128)S(1)}, f32[256,256]{1,0:T(8,128)}, u32[]{:S(2)}) copy-start(f32[256,256]{1,0:T(8,128)} %param.11) | copy-start | bytes 786436
  115.9 345.2 %all-reduce.7.cloned.1.call-start = ((), (), s32[]{:S(2)}) async-start(), calls=%async_computation.1 | async-start | bytes 1048576 | tf_op jit(solution)/shard_map/psum | solution.py:70
  118.7 127.1 %copy-start.4 = (f32[512,256]{1,0:T(8,128)S(1)}, f32[512,256]{1,0:T(8,128)}, u32[]{:S(2)}) copy-start(f32[512,256]{1,0:T(8,128)} %param.8) | copy-start | bytes 1572868
  126.9 83.9 %collective-permute-start.11 = (f32[512,256]{1,0:T(8,128)}, f32[512,256]{1,0:T(8,128)}, u32[]{:S(2)}, u32[]{:S(2)}) collective-permute-start(f32[512,256]{1,0:T(8,128)} %get-tuple-element.12), channel_id=1, source_target_pairs={{0,96},{16,112},{32,128},{48,144},{64,160},{80,176},{96,192},{112,... | collective-permute-start | bytes 1572872 | tf_op jit(solution)/shard_map/ppermute | solution.py:14
  130.7 80.1 %collective-permute-start.10 = (f32[512,256]{1,0:T(8,128)}, f32[512,256]{1,0:T(8,128)}, u32[]{:S(2)}, u32[]{:S(2)}) collective-permute-start(f32[512,256]{1,0:T(8,128)} %get-tuple-element.13), channel_id=1, source_target_pairs={{0,80},{16,96},{32,112},{48,128},{64,144},{80,160},{96,176},{112,1... | collective-permute-start | bytes 1572872 | tf_op jit(solution)/shard_map/ppermute | solution.py:14
  132.7 89.3 %collective-permute-start.9 = (f32[512,256]{1,0:T(8,128)S(1)}, f32[512,256]{1,0:T(8,128)}, u32[]{:S(2)}, u32[]{:S(2)}) collective-permute-start(f32[512,256]{1,0:T(8,128)S(1)} %get-tuple-element.14), channel_id=1, source_target_pairs={{0,64},{16,80},{32,96},{48,112},{64,128},{80,144},{96,160},{112,17... | collective-permute-start | bytes 1572872 | tf_op jit(solution)/shard_map/ppermute | solution.py:14
  134.6 99.7 %collective-permute-start.8 = (f32[512,256]{1,0:T(8,128)S(1)}, f32[512,256]{1,0:T(8,128)}, u32[]{:S(2)}, u32[]{:S(2)}) collective-permute-start(f32[512,256]{1,0:T(8,128)S(1)} %get-tuple-element.15), channel_id=1, source_target_pairs={{0,48},{16,64},{32,80},{48,96},{64,112},{80,128},{96,144},{112,160... | collective-permute-start | bytes 1572872 | tf_op jit(solution)/shard_map/ppermute | solution.py:14
  136.5 109.3 %collective-permute-start.7 = (f32[512,256]{1,0:T(8,128)S(1)}, f32[512,256]{1,0:T(8,128)}, u32[]{:S(2)}, u32[]{:S(2)}) collective-permute-start(f32[512,256]{1,0:T(8,128)S(1)} %get-tuple-element.16), channel_id=1, source_target_pairs={{0,32},{16,48},{32,64},{48,80},{64,96},{80,112},{96,128},{112,144}... | collective-permute-start | bytes 1572872 | tf_op jit(solution)/shard_map/ppermute | solution.py:14
  209.0 58.8 %slice-start = ((s8[7340032]{0:T(1024)(128)(4,1)}), s8[4194304]{0:T(1024)(128)(4,1)S(1)}, s32[]{:S(2)}) async-start(s8[7340032]{0:T(1024)(128)(4,1)} %bitcast.16), calls=%async_computation.2 | async-start | bytes 8388608
  210.8 57.0 %slice-start.1 = ((s8[7340032]{0:T(1024)(128)(4,1)}), s8[3145728]{0:T(1024)(128)(4,1)S(1)}, s32[]{:S(2)}) async-start(s8[7340032]{0:T(1024)(128)(4,1)} %bitcast.16), calls=%async_computation.3 | async-start | bytes 6291456
  257.0 109.7 %collective-permute-start.17 = (f32[512,256]{1,0:T(8,128)S(1)}, f32[512,256]{1,0:T(8,128)}, u32[]{:S(2)}, u32[]{:S(2)}) collective-permute-start(f32[512,256]{1,0:T(8,128)S(1)} %get-tuple-element.18), channel_id=1, source_target_pairs={{96,0},{112,16},{128,32},{144,48},{160,64},{176,80},{192,96},{208,... | collective-permute-start | bytes 1572872 | tf_op jit(solution)/shard_map/ppermute | solution.py:14
  258.9 109.7 %collective-permute-start.16 = (f32[512,256]{1,0:T(8,128)S(1)}, f32[512,256]{1,0:T(8,128)}, u32[]{:S(2)}, u32[]{:S(2)}) collective-permute-start(f32[512,256]{1,0:T(8,128)S(1)} %get-tuple-element.18), channel_id=1, source_target_pairs={{80,0},{96,16},{112,32},{128,48},{144,64},{160,80},{176,96},{192,1... | collective-permute-start | bytes 1572872 | tf_op jit(solution)/shard_map/ppermute | solution.py:14
  260.8 102.1 %collective-permute-start.14 = (f32[512,256]{1,0:T(8,128)S(1)}, f32[512,256]{1,0:T(8,128)}, u32[]{:S(2)}, u32[]{:S(2)}) collective-permute-start(f32[512,256]{1,0:T(8,128)S(1)} %get-tuple-element.18), channel_id=1, source_target_pairs={{48,0},{64,16},{80,32},{96,48},{112,64},{128,80},{144,96},{160,112... | collective-permute-start | bytes 1572872 | tf_op jit(solution)/shard_map/ppermute | solution.py:14
  263.4 84.4 %collective-permute-start.13 = (f32[512,256]{1,0:T(8,128)S(1)}, f32[512,256]{1,0:T(8,128)S(1)}, u32[]{:S(2)}, u32[]{:S(2)}) collective-permute-start(f32[512,256]{1,0:T(8,128)S(1)} %get-tuple-element.18), channel_id=1, source_target_pairs={{32,0},{48,16},{64,32},{80,48},{96,64},{112,80},{128,96},{144,112}... | collective-permute-start | bytes 1572872 | tf_op jit(solution)/shard_map/ppermute | solution.py:14
  265.4 89.0 %collective-permute-start.12 = (f32[512,256]{1,0:T(8,128)S(1)}, f32[512,256]{1,0:T(8,128)S(1)}, u32[]{:S(2)}, u32[]{:S(2)}) collective-permute-start(f32[512,256]{1,0:T(8,128)S(1)} %get-tuple-element.18), channel_id=1, source_target_pairs={{16,0},{32,16},{48,32},{64,48},{80,64},{96,80},{112,96},{128,112},... | collective-permute-start | bytes 1572872 | tf_op jit(solution)/shard_map/ppermute | solution.py:14
  280.4 1.9 copy-start.2
  347.9 6.5 %copy-start.8 = (f32[512,256]{1,0:T(8,128)}, f32[512,256]{1,0:T(8,128)S(1)}, u32[]{:S(2)}) copy-start(f32[512,256]{1,0:T(8,128)S(1)} %collective-permute-done.13) | copy-start | bytes 1572868
  347.9 25.5 %collective-permute-start.15 = (f32[512,256]{1,0:T(8,128)S(1)}, f32[512,256]{1,0:T(8,128)}, u32[]{:S(2)}, u32[]{:S(2)}) collective-permute-start(f32[512,256]{1,0:T(8,128)S(1)} %get-tuple-element.18), channel_id=1, source_target_pairs={{64,0},{80,16},{96,32},{112,48},{128,64},{144,80},{160,96},{176,11... | collective-permute-start | bytes 1572872 | tf_op jit(solution)/shard_map/ppermute | solution.py:14
  354.3 0.8 copy-start.9
  355.1 20.2 %collective-permute-start.18 = (f32[512,256]{1,0:T(8,128)}, f32[512,256]{1,0:T(8,128)S(1)}, u32[]{:S(2)}, u32[]{:S(2)}) collective-permute-start(f32[512,256]{1,0:T(8,128)} %get-tuple-element.5), channel_id=1, source_target_pairs={{0,16},{16,32},{32,48},{48,64},{64,80},{80,96},{96,112},{112,128},... | collective-permute-start | bytes 1572872 | tf_op jit(solution)/shard_map/ppermute | solution.py:14
  362.9 99.9 %collective-permute-start.23 = (f32[512,256]{1,0:T(8,128)}, f32[512,256]{1,0:T(8,128)}, u32[]{:S(2)}, u32[]{:S(2)}) collective-permute-start(f32[512,256]{1,0:T(8,128)} %get-tuple-element.6), channel_id=1, source_target_pairs={{0,96},{16,112},{32,128},{48,144},{64,160},{80,176},{96,192},{112,... | collective-permute-start | bytes 1572872 | tf_op jit(solution)/shard_map/ppermute | solution.py:14
  366.7 96.1 %collective-permute-start.22 = (f32[512,256]{1,0:T(8,128)}, f32[512,256]{1,0:T(8,128)}, u32[]{:S(2)}, u32[]{:S(2)}) collective-permute-start(f32[512,256]{1,0:T(8,128)} %get-tuple-element.7), channel_id=1, source_target_pairs={{0,80},{16,96},{32,112},{48,128},{64,144},{80,160},{96,176},{112,1... | collective-permute-start | bytes 1572872 | tf_op jit(solution)/shard_map/ppermute | solution.py:14
  368.6 94.2 %collective-permute-start.21 = (f32[512,256]{1,0:T(8,128)}, f32[512,256]{1,0:T(8,128)}, u32[]{:S(2)}, u32[]{:S(2)}) collective-permute-start(f32[512,256]{1,0:T(8,128)} %get-tuple-element.8), channel_id=1, source_target_pairs={{0,64},{16,80},{32,96},{48,112},{64,128},{80,144},{96,160},{112,17... | collective-permute-start | bytes 1572872 | tf_op jit(solution)/shard_map/ppermute | solution.py:14
  373.4 97.0 %collective-permute-start.20 = (f32[512,256]{1,0:T(8,128)S(1)}, f32[512,256]{1,0:T(8,128)}, u32[]{:S(2)}, u32[]{:S(2)}) collective-permute-start(f32[512,256]{1,0:T(8,128)S(1)} %get-tuple-element.9), channel_id=1, source_target_pairs={{0,48},{16,64},{32,80},{48,96},{64,112},{80,128},{96,144},{112,160... | collective-permute-start | bytes 1572872 | tf_op jit(solution)/shard_map/ppermute | solution.py:14
  375.3 10.5 %copy-start.6 = (f32[512,256]{1,0:T(8,128)}, f32[512,256]{1,0:T(8,128)S(1)}, u32[]{:S(2)}) copy-start(f32[512,256]{1,0:T(8,128)S(1)} %collective-permute-done.18) | copy-start | bytes 1572868
  375.4 111.8 %collective-permute-start.19 = (f32[512,256]{1,0:T(8,128)S(1)}, f32[512,256]{1,0:T(8,128)}, u32[]{:S(2)}, u32[]{:S(2)}) collective-permute-start(f32[512,256]{1,0:T(8,128)S(1)} %get-tuple-element.10), channel_id=1, source_target_pairs={{0,32},{16,48},{32,64},{48,80},{64,96},{80,112},{96,128},{112,144}... | collective-permute-start | bytes 1572872 | tf_op jit(solution)/shard_map/ppermute | solution.py:14
Sparse Core Ops, SparseCore 0:
  116.0 92.9 all-reduce.4
  359.2 101.8 all-reduce.6
where the time goes:
time: 513 us; the launch traced here: 505 us
  waiting for transfers between devices  314 us (61%)
  starting transfers between devices  56.2 us (11%)
  matrix products  55.7 us (11%)
  local copies, waits for them, and re-layouts  54.2 us (11%)
  between operations  14.1 us (3%)
  other arithmetic  11.7 us (2%)
    ppermute x24, waiting for transfers between devices, passed_along(): return lax.ppermute(block, axis, route)  173 us
    psum x2, waiting for transfers between devices, body(): scores = lax.psum(partial_scores, 'trait')  140 us
    ppermute x24, starting transfers between devices, passed_along(): return lax.ppermute(block, axis, route)  56.1 us
    dot_general x2, matrix products, body(): lax.dot_general(sheared, effects, (((0,), (0,)), ((), ())), precision=lax...  27.2 us
    unnamed x35, local copies, waits for them, and re-layouts  24.4 us
    dot_general x2, matrix products, body(): jnp.dot(sheared, window, precision=lax.Precision.HIGHEST, preferred_eleme...  22.3 us
    reshape x1, local copies, waits for them, and re-layouts, shear(): padded.reshape(-1)  11.3 us
  transfers between devices with their start and end apart: 26, of which 13 were waited for; matrix products, arithmetic and copies ran while one was open for 19% of the time, Pallas kernels for 0%

commit v1 on v0

--- a/solution.py
+++ b/solution.py
@@ -67,7 +67,7 @@
         partial_scores = jnp.dot(
             effects, factor_in, precision=lax.Precision.HIGHEST, preferred_element_type=jnp.float32
         )
-        scores = lax.psum(partial_scores, "trait")
+        scores = jnp.sum(lax.all_gather(partial_scores, "trait"), axis=0)
         projected = lax.dot_general(
             scores,
             factor_out,

time: 513 us -> 487 us (0.949)
  waiting for transfers between devices: 314 us -> 297 us
  local copies, waits for them, and re-layouts: 54.2 us -> 41.3 us
  other arithmetic: 11.7 us -> 19.5 us
    psum x2 -> x0, waiting for transfers between devices: 140 us -> none  [body(): scores = lax.psum(partial_scores, 'trait')]
    ppermute x24, waiting for transfers between devices: 173 us -> 297 us  [passed_along(): return lax.ppermute(block, axis, route)]
    unnamed x35 -> x29, local copies, waits for them, and re-layouts: 24.4 us -> 13.5 us
    reduce_sum x0 -> x2, other arithmetic: none -> 8.03 us  [body(): scores = jnp.sum(lax.all_gather(partial_scores, 'trait'), axis=0)]
  transfers between devices with their start and end apart: 26 -> 26, of which waited for: 13 -> 15; matrix products, arithmetic and copies ran while one was open for 19% -> 19% of each run, Pallas kernels for 0% -> 0%
where the time goes in v1:
time: 487 us; the launch traced here: 483 us
  waiting for transfers between devices  297 us (61%)
  matrix products  56.9 us (12%)
  starting transfers between devices  55 us (11%)
  local copies, waits for them, and re-layouts  41.3 us (8%)
  other arithmetic  19.5 us (4%)
  between operations  13.8 us (3%)
    ppermute x24, waiting for transfers between devices, passed_along(): return lax.ppermute(block, axis, route)  297 us
    ppermute x24, starting transfers between devices, passed_along(): return lax.ppermute(block, axis, route)  54.9 us
    dot_general x2, matrix products, body(): lax.dot_general(sheared, effects, (((0,), (0,)), ((), ())), precision=lax...  29.2 us
    dot_general x2, matrix products, body(): jnp.dot(sheared, window, precision=lax.Precision.HIGHEST, preferred_eleme...  22.6 us
    unnamed x29, local copies, waits for them, and re-layouts  13.5 us
    reshape x1, local copies, waits for them, and re-layouts, shear(): padded.reshape(-1)  11.3 us
  transfers between devices with their start and end apart: 26, of which 15 were waited for; matrix products, arithmetic and copies ran while one was open for 19% of the time, Pallas kernels for 0%

profile of v1, /device:TPU:147, one launch (start us, length us, event | category | flops | bytes accessed | tf_op | source)
XLA Modules:
  0.0 483.3 jit_solution(2155216629171249581)
XLA Ops:
  6.5 2.0 collective-permute-start.5
  8.6 1.9 collective-permute-start.4
  10.5 2.3 collective-permute-start.2
  12.8 1.9 collective-permute-start.1
  14.8 2.3 collective-permute-start
  17.1 2.4 fusion.26
  21.1 3.7 fusion
  24.9 3.6 pad.5
  28.4 11.3 %reshape.18 = f32[1835520]{0:T(1024)} reshape(f32[512,3585]{1,0:T(8,128)} %pad.5) | data formatting | bytes 14684160 | tf_op jit(solution)/shard_map/reshape | solution.py:32
  39.7 6.3 %pad_maximum_fusion = f32[1835008]{0:T(1024)} fusion(f32[1835520]{0:T(1024)} %reshape.18, f32[1]{0:T(128)} %constant.8.clone.1), kind=kLoop, calls=%fused_computation | loop fusion | flops 1835008 | bytes 14682116 | tf_op jit(solution)/shard_map/concatenate | solution.py:32
  46.0 8.4 %reshape.19 = f32[512,3584]{1,0:T(8,128)} reshape(f32[1835008]{0:T(1024)} %pad_maximum_fusion) | data formatting | bytes 14680064 | tf_op jit(solution)/shard_map/reshape | solution.py:33
  54.3 14.6 %fusion.25 = f32[3584,256]{1,0:T(8,128)S(1)} fusion(f32[512,3584]{1,0:T(8,128)} %reshape.19, f32[512,256]{1,0:T(8,128)S(1)} %copy-done.3), kind=kOutput, calls=%fused_computation.51 | convolution fusion | flops 5637144576 | bytes 11534336 | tf_op jit(solution)/shard_map/dot_general | solution.py:53
  69.0 1.4 fusion.24
  70.4 29.0 %collective-permute-done.1 = f32[512,256]{1,0:T(8,128)S(1)} collective-permute-done((f32[512,256]{1,0:T(8,128)}, f32[512,256]{1,0:T(8,128)S(1)}, u32[]{:S(2)}, u32[]{:S(2)}) %collective-permute-start.1) | collective-permute-done | bytes 524320 | tf_op jit(solution)/shard_map/ppermute | solution.py:14
  99.4 2.7 collective-permute-start.3
  102.1 3.9 collective-permute-done
  106.0 2.2 collective-permute-start.6
  108.2 0.8 constant_dynamic-update-slice_fusion.6
  109.1 1.9 constant_dynamic-update-slice_fusion.5
  110.9 1.9 constant_dynamic-update-slice_fusion.4
  112.8 1.9 collective-permute-start.11
  114.7 1.9 constant_dynamic-update-slice_fusion.3
  116.7 1.9 collective-permute-start.10
  118.6 1.9 collective-permute-start.9
  120.5 5.9 %collective-permute-done.3 = f32[512,256]{1,0:T(8,128)S(1)} collective-permute-done((f32[512,256]{1,0:T(8,128)S(1)}, f32[512,256]{1,0:T(8,128)S(1)}, u32[]{:S(2)}, u32[]{:S(2)}) %collective-permute-start.3) | collective-permute-done | bytes 524320 | tf_op jit(solution)/shard_map/ppermute | solution.py:14
  126.4 1.9 collective-permute-start.8
  128.3 2.6 collective-permute-start.7
  131.0 0.9 constant_dynamic-update-slice_fusion.2
  131.8 1.9 constant_dynamic-update-slice_fusion.1
  134.5 4.0 reduce_sum.28
  139.2 27.2 %collective-permute-done.10 = f32[512,256]{1,0:T(8,128)} collective-permute-done((f32[512,256]{1,0:T(8,128)}, f32[512,256]{1,0:T(8,128)}, u32[]{:S(2)}, u32[]{:S(2)}) %collective-permute-start.10) | collective-permute-done | bytes 524320 | tf_op jit(solution)/shard_map/ppermute | solution.py:14
  166.4 41.3 %collective-permute-done.9 = f32[512,256]{1,0:T(8,128)} collective-permute-done((f32[512,256]{1,0:T(8,128)}, f32[512,256]{1,0:T(8,128)}, u32[]{:S(2)}, u32[]{:S(2)}) %collective-permute-start.9) | collective-permute-done | bytes 524320 | tf_op jit(solution)/shard_map/ppermute | solution.py:14
  207.7 12.2 %collective-permute-done.8 = f32[512,256]{1,0:T(8,128)} collective-permute-done((f32[512,256]{1,0:T(8,128)S(1)}, f32[512,256]{1,0:T(8,128)}, u32[]{:S(2)}, u32[]{:S(2)}) %collective-permute-start.8) | collective-permute-done | bytes 524320 | tf_op jit(solution)/shard_map/ppermute | solution.py:14
  219.9 16.7 %collective-permute-done.7 = f32[512,256]{1,0:T(8,128)} collective-permute-done((f32[512,256]{1,0:T(8,128)S(1)}, f32[512,256]{1,0:T(8,128)}, u32[]{:S(2)}, u32[]{:S(2)}) %collective-permute-start.7) | collective-permute-done | bytes 524320 | tf_op jit(solution)/shard_map/ppermute | solution.py:14
  236.6 11.4 %constant_dynamic-update-slice_fusion.13 = (f32[3584,256]{1,0:T(8,128)}, f32[512,256]{1,0:T(8,128)S(1)}) fusion(f32[512,256]{1,0:T(8,128)S(1)} %copy-done.3, f32[512,256]{1,0:T(8,128)S(1)} %fusion.2, f32[512,256]{1,0:T(8,128)S(1)} %copy-done.4, f32[512,256]{1,0:T(8,128)} %collective-permute-done.11, f32[512,256]{1,0:T(8,128)} %collective-permute-done.10, ...), kind=kOutput, calls=%fused_computation.46 | convolution fusion | flops 5638717440 | bytes 17301504 | tf_op jit(solution)/shard_map/dot_general | solution.py:50
  248.0 1.4 fusion.28
  249.4 1.9 collective-permute-start.17
  251.4 1.9 collective-permute-start.16
  253.3 1.9 collective-permute-start.14
  255.2 1.9 collective-permute-start.13
  257.1 1.9 collective-permute-start.12
  259.1 14.6 %fusion.27 = f32[3584,256]{1,0:T(8,128)S(1)} fusion(f32[512,3584]{1,0:T(8,128)} %reshape.19, f32[512,256]{1,0:T(8,128)S(1)} %get-tuple-element.18), kind=kOutput, calls=%fused_computation.53 | convolution fusion | flops 5637144576 | bytes 11534336 | tf_op jit(solution)/shard_map/dot_general | solution.py:53
  273.7 1.6 fusion.23
  275.3 61.4 %collective-permute-done.13 = f32[512,256]{1,0:T(8,128)S(1)} collective-permute-done((f32[512,256]{1,0:T(8,128)S(1)}, f32[512,256]{1,0:T(8,128)S(1)}, u32[]{:S(2)}, u32[]{:S(2)}) %collective-permute-start.13) | collective-permute-done | bytes 524320 | tf_op jit(solution)/shard_map/ppermute | solution.py:14
  336.7 4.7 collective-permute-start.15
  341.8 1.9 collective-permute-start.18
  343.7 0.8 constant_dynamic-update-slice_fusion.12
  345.3 1.9 collective-permute-start.23
  347.3 0.8 constant_dynamic-update-slice_fusion.10
  348.1 1.9 collective-permute-start.22
  350.0 1.9 collective-permute-start.21
  352.0 9.3 %collective-permute-done.15 = f32[512,256]{1,0:T(8,128)S(1)} collective-permute-done((f32[512,256]{1,0:T(8,128)S(1)}, f32[512,256]{1,0:T(8,128)S(1)}, u32[]{:S(2)}, u32[]{:S(2)}) %collective-permute-start.15) | collective-permute-done | bytes 524320 | tf_op jit(solution)/shard_map/ppermute | solution.py:14
  361.3 1.9 collective-permute-start.20
  363.2 5.4 %collective-permute-start.19 = (f32[512,256]{1,0:T(8,128)S(1)}, f32[512,256]{1,0:T(8,128)}, u32[]{:S(2)}, u32[]{:S(2)}) collective-permute-start(f32[512,256]{1,0:T(8,128)S(1)} %get-tuple-element.10), channel_id=1, source_target_pairs={{0,32},{16,48},{32,64},{48,80},{64,96},{80,112},{96,128},{112,144}... | collective-permute-start | bytes 1572872 | tf_op jit(solution)/shard_map/ppermute | solution.py:14
  368.6 0.8 constant_dynamic-update-slice_fusion.9
  369.5 0.8 constant_dynamic-update-slice_fusion.8
  370.3 0.8 constant_dynamic-update-slice_fusion.7
  371.2 4.0 reduce_sum.29
  375.8 27.2 %collective-permute-done.23 = f32[512,256]{1,0:T(8,128)} collective-permute-done((f32[512,256]{1,0:T(8,128)}, f32[512,256]{1,0:T(8,128)}, u32[]{:S(2)}, u32[]{:S(2)}) %collective-permute-start.23) | collective-permute-done | bytes 524320 | tf_op jit(solution)/shard_map/ppermute | solution.py:14
  403.0 24.3 %collective-permute-done.22 = f32[512,256]{1,0:T(8,128)} collective-permute-done((f32[512,256]{1,0:T(8,128)}, f32[512,256]{1,0:T(8,128)}, u32[]{:S(2)}, u32[]{:S(2)}) %collective-permute-start.22) | collective-permute-done | bytes 524320 | tf_op jit(solution)/shard_map/ppermute | solution.py:14
  427.3 18.2 %collective-permute-done.21 = f32[512,256]{1,0:T(8,128)} collective-permute-done((f32[512,256]{1,0:T(8,128)}, f32[512,256]{1,0:T(8,128)}, u32[]{:S(2)}, u32[]{:S(2)}) %collective-permute-start.21) | collective-permute-done | bytes 524320 | tf_op jit(solution)/shard_map/ppermute | solution.py:14
  445.4 6.2 %collective-permute-done.20 = f32[512,256]{1,0:T(8,128)} collective-permute-done((f32[512,256]{1,0:T(8,128)}, f32[512,256]{1,0:T(8,128)}, u32[]{:S(2)}, u32[]{:S(2)}) %collective-permute-start.20) | collective-permute-done | bytes 524320 | tf_op jit(solution)/shard_map/ppermute | solution.py:14
  451.6 13.6 %collective-permute-done.19 = f32[512,256]{1,0:T(8,128)} collective-permute-done((f32[512,256]{1,0:T(8,128)S(1)}, f32[512,256]{1,0:T(8,128)}, u32[]{:S(2)}, u32[]{:S(2)}) %collective-permute-start.19) | collective-permute-done | bytes 524320 | tf_op jit(solution)/shard_map/ppermute | solution.py:14
  465.2 11.2 %fusion.7 = f32[512,256]{1,0:T(8,128)} fusion(f32[512,256]{1,0:T(8,128)S(1)} %get-tuple-element.18, f32[512,256]{1,0:T(8,128)S(1)} %fusion.1, f32[512,256]{1,0:T(8,128)S(1)} %copy-done.4, f32[512,3584]{1,0:T(8,128)} %reshape.19, f32[3584,256]{1,0:T(8,128)} %constant_dynamic-update-slice_fusion.7, f32[512,256]{1,0:T(8,128)} %collective-permute-done.23, ...), kind=kOutput, calls=%fused_computation.12 | convolution fusion | flops 5638717440 | bytes 16777216 | tf_op jit(solution)/shard_map/dot_general | solution.py:50
  (43 shorter events, 4.9 us)
Async XLA Ops:
  6.5 10.5 %copy-start = (f32[256,256]{1,0:T(8,128)S(1)}, f32[256,256]{1,0:T(8,128)}, u32[]{:S(2)}) copy-start(f32[256,256]{1,0:T(8,128)} %param.10) | copy-start | bytes 786436
  6.5 128.0 %all-gather.5.cloned.1.call-start = ((), (), s32[]{:S(2)}) async-start(), calls=%async_computation | async-start | bytes 8912896 | tf_op jit(solution)/shard_map/all_gather | solution.py:70
  6.5 110.1 %collective-permute-start.5 = (f32[512,256]{1,0:T(8,128)}, f32[512,256]{1,0:T(8,128)S(1)}, u32[]{:S(2)}, u32[]{:S(2)}) collective-permute-start(f32[512,256]{1,0:T(8,128)} %param.9), channel_id=1, source_target_pairs={{96,0},{112,16},{128,32},{144,48},{160,64},{176,80},{192,96},{208,... | collective-permute-start | bytes 1572872 | tf_op jit(solution)/shard_map/ppermute | solution.py:14
  8.6 110.0 %collective-permute-start.4 = (f32[512,256]{1,0:T(8,128)}, f32[512,256]{1,0:T(8,128)}, u32[]{:S(2)}, u32[]{:S(2)}) collective-permute-start(f32[512,256]{1,0:T(8,128)} %param.9), channel_id=1, source_target_pairs={{80,0},{96,16},{112,32},{128,48},{144,64},{160,80},{176,96},{192,1... | collective-permute-start | bytes 1572872 | tf_op jit(solution)/shard_map/ppermute | solution.py:14
  10.5 102.3 %collective-permute-start.2 = (f32[512,256]{1,0:T(8,128)}, f32[512,256]{1,0:T(8,128)}, u32[]{:S(2)}, u32[]{:S(2)}) collective-permute-start(f32[512,256]{1,0:T(8,128)} %param.9), channel_id=1, source_target_pairs={{48,0},{64,16},{80,32},{96,48},{112,64},{128,80},{144,96},{160,112... | collective-permute-start | bytes 1572872 | tf_op jit(solution)/shard_map/ppermute | solution.py:14
  12.8 86.6 %collective-permute-start.1 = (f32[512,256]{1,0:T(8,128)}, f32[512,256]{1,0:T(8,128)S(1)}, u32[]{:S(2)}, u32[]{:S(2)}) collective-permute-start(f32[512,256]{1,0:T(8,128)} %param.9), channel_id=1, source_target_pairs={{32,0},{48,16},{64,32},{80,48},{96,64},{112,80},{128,96},{144,112}... | collective-permute-start | bytes 1572872 | tf_op jit(solution)/shard_map/ppermute | solution.py:14
  14.8 91.3 %collective-permute-start = (f32[512,256]{1,0:T(8,128)}, f32[512,256]{1,0:T(8,128)}, u32[]{:S(2)}, u32[]{:S(2)}) collective-permute-start(f32[512,256]{1,0:T(8,128)} %param.9), channel_id=1, source_target_pairs={{16,0},{32,16},{48,32},{64,48},{80,64},{96,80},{112,96},{128,112},... | collective-permute-start | bytes 1572872 | tf_op jit(solution)/shard_map/ppermute | solution.py:14
  19.5 351.6 %all-gather.7.cloned.1.call-start = ((), (), s32[]{:S(2)}) async-start(), calls=%async_computation.1 | async-start | bytes 8912896 | tf_op jit(solution)/shard_map/all_gather | solution.py:70
  46.0 8.4 %copy-start.3 = (f32[512,256]{1,0:T(8,128)S(1)}, f32[512,256]{1,0:T(8,128)}, u32[]{:S(2)}) copy-start(f32[512,256]{1,0:T(8,128)} %param.9) | copy-start | bytes 1572868
  69.0 40.1 %copy-start.2 = (f32[3584,256]{1,0:T(8,128)}, f32[3584,256]{1,0:T(8,128)S(1)}, u32[]{:S(2)}) copy-start(f32[3584,256]{1,0:T(8,128)S(1)} %fusion.25) | copy-start | bytes 11010052
  99.4 6.6 %copy-start.8 = (f32[512,256]{1,0:T(8,128)}, f32[512,256]{1,0:T(8,128)S(1)}, u32[]{:S(2)}) copy-start(f32[512,256]{1,0:T(8,128)S(1)} %collective-permute-done.1) | copy-start | bytes 1572868
  99.4 27.0 %collective-permute-start.3 = (f32[512,256]{1,0:T(8,128)S(1)}, f32[512,256]{1,0:T(8,128)S(1)}, u32[]{:S(2)}, u32[]{:S(2)}) collective-permute-start(f32[512,256]{1,0:T(8,128)S(1)} %copy-done.3), channel_id=1, source_target_pairs={{64,0},{80,16},{96,32},{112,48},{128,64},{144,80},{160,96},{176,11... | collective-permute-start | bytes 1572872 | tf_op jit(solution)/shard_map/ppermute | solution.py:14
  106.0 22.3 %collective-permute-start.6 = (f32[512,256]{1,0:T(8,128)S(1)}, f32[512,256]{1,0:T(8,128)S(1)}, u32[]{:S(2)}, u32[]{:S(2)}) collective-permute-start(f32[512,256]{1,0:T(8,128)S(1)} %get-tuple-element.11), channel_id=1, source_target_pairs={{0,16},{16,32},{32,48},{48,64},{64,80},{80,96},{96,112},{112,128},... | collective-permute-start | bytes 1572872 | tf_op jit(solution)/shard_map/ppermute | solution.py:14
  112.8 26.4 %collective-permute-start.11 = (f32[512,256]{1,0:T(8,128)}, f32[512,256]{1,0:T(8,128)}, u32[]{:S(2)}, u32[]{:S(2)}) collective-permute-start(f32[512,256]{1,0:T(8,128)} %get-tuple-element.12), channel_id=1, source_target_pairs={{0,96},{16,112},{32,128},{48,144},{64,160},{80,176},{96,192},{112,... | collective-permute-start | bytes 1572872 | tf_op jit(solution)/shard_map/ppermute | solution.py:14
  116.7 49.7 %collective-permute-start.10 = (f32[512,256]{1,0:T(8,128)}, f32[512,256]{1,0:T(8,128)}, u32[]{:S(2)}, u32[]{:S(2)}) collective-permute-start(f32[512,256]{1,0:T(8,128)} %get-tuple-element.13), channel_id=1, source_target_pairs={{0,80},{16,96},{32,112},{48,128},{64,144},{80,160},{96,176},{112,1... | collective-permute-start | bytes 1572872 | tf_op jit(solution)/shard_map/ppermute | solution.py:14
  118.6 89.1 %collective-permute-start.9 = (f32[512,256]{1,0:T(8,128)}, f32[512,256]{1,0:T(8,128)}, u32[]{:S(2)}, u32[]{:S(2)}) collective-permute-start(f32[512,256]{1,0:T(8,128)} %get-tuple-element.14), channel_id=1, source_target_pairs={{0,64},{16,80},{32,96},{48,112},{64,128},{80,144},{96,160},{112,17... | collective-permute-start | bytes 1572872 | tf_op jit(solution)/shard_map/ppermute | solution.py:14
  126.4 93.5 %collective-permute-start.8 = (f32[512,256]{1,0:T(8,128)S(1)}, f32[512,256]{1,0:T(8,128)}, u32[]{:S(2)}, u32[]{:S(2)}) collective-permute-start(f32[512,256]{1,0:T(8,128)S(1)} %get-tuple-element.15), channel_id=1, source_target_pairs={{0,48},{16,64},{32,80},{48,96},{64,112},{80,128},{96,144},{112,160... | collective-permute-start | bytes 1572872 | tf_op jit(solution)/shard_map/ppermute | solution.py:14
  128.3 6.2 %copy-start.7 = (f32[512,256]{1,0:T(8,128)}, f32[512,256]{1,0:T(8,128)S(1)}, u32[]{:S(2)}) copy-start(f32[512,256]{1,0:T(8,128)S(1)} %collective-permute-done.6) | copy-start | bytes 1572868
  128.3 108.3 %collective-permute-start.7 = (f32[512,256]{1,0:T(8,128)S(1)}, f32[512,256]{1,0:T(8,128)}, u32[]{:S(2)}, u32[]{:S(2)}) collective-permute-start(f32[512,256]{1,0:T(8,128)S(1)} %get-tuple-element.16), channel_id=1, source_target_pairs={{0,32},{16,48},{32,64},{48,80},{64,96},{80,112},{96,128},{112,144}... | collective-permute-start | bytes 1572872 | tf_op jit(solution)/shard_map/ppermute | solution.py:14
  134.5 4.1 copy-start.5
  134.5 102.1 %copy-start.4 = (f32[512,256]{1,0:T(8,128)S(1)}, f32[512,256]{1,0:T(8,128)}, u32[]{:S(2)}) copy-start(f32[512,256]{1,0:T(8,128)} %param.8) | copy-start | bytes 1572868
  249.4 98.7 %collective-permute-start.17 = (f32[512,256]{1,0:T(8,128)S(1)}, f32[512,256]{1,0:T(8,128)S(1)}, u32[]{:S(2)}, u32[]{:S(2)}) collective-permute-start(f32[512,256]{1,0:T(8,128)S(1)} %get-tuple-element.18), channel_id=1, source_target_pairs={{96,0},{112,16},{128,32},{144,48},{160,64},{176,80},{192,96},{208,... | collective-permute-start | bytes 1572872 | tf_op jit(solution)/shard_map/ppermute | solution.py:14
  251.4 98.7 %collective-permute-start.16 = (f32[512,256]{1,0:T(8,128)S(1)}, f32[512,256]{1,0:T(8,128)S(1)}, u32[]{:S(2)}, u32[]{:S(2)}) collective-permute-start(f32[512,256]{1,0:T(8,128)S(1)} %get-tuple-element.18), channel_id=1, source_target_pairs={{80,0},{96,16},{112,32},{128,48},{144,64},{160,80},{176,96},{192,1... | collective-permute-start | bytes 1572872 | tf_op jit(solution)/shard_map/ppermute | solution.py:14
  253.3 92.1 %collective-permute-start.14 = (f32[512,256]{1,0:T(8,128)S(1)}, f32[512,256]{1,0:T(8,128)S(1)}, u32[]{:S(2)}, u32[]{:S(2)}) collective-permute-start(f32[512,256]{1,0:T(8,128)S(1)} %get-tuple-element.18), channel_id=1, source_target_pairs={{48,0},{64,16},{80,32},{96,48},{112,64},{128,80},{144,96},{160,112... | collective-permute-start | bytes 1572872 | tf_op jit(solution)/shard_map/ppermute | solution.py:14
  255.2 81.5 %collective-permute-start.13 = (f32[512,256]{1,0:T(8,128)S(1)}, f32[512,256]{1,0:T(8,128)S(1)}, u32[]{:S(2)}, u32[]{:S(2)}) collective-permute-start(f32[512,256]{1,0:T(8,128)S(1)} %get-tuple-element.18), channel_id=1, source_target_pairs={{32,0},{48,16},{64,32},{80,48},{96,64},{112,80},{128,96},{144,112}... | collective-permute-start | bytes 1572872 | tf_op jit(solution)/shard_map/ppermute | solution.py:14
  257.1 84.6 %collective-permute-start.12 = (f32[512,256]{1,0:T(8,128)S(1)}, f32[512,256]{1,0:T(8,128)S(1)}, u32[]{:S(2)}, u32[]{:S(2)}) collective-permute-start(f32[512,256]{1,0:T(8,128)S(1)} %get-tuple-element.18), channel_id=1, source_target_pairs={{16,0},{32,16},{48,32},{64,48},{80,64},{96,80},{112,96},{128,112},... | collective-permute-start | bytes 1572872 | tf_op jit(solution)/shard_map/ppermute | solution.py:14
  273.7 70.8 %copy-start.1 = (f32[3584,256]{1,0:T(8,128)}, f32[3584,256]{1,0:T(8,128)S(1)}, u32[]{:S(2)}) copy-start(f32[3584,256]{1,0:T(8,128)S(1)} %fusion.27) | copy-start | bytes 11010052
  336.7 24.6 %collective-permute-start.15 = (f32[512,256]{1,0:T(8,128)S(1)}, f32[512,256]{1,0:T(8,128)S(1)}, u32[]{:S(2)}, u32[]{:S(2)}) collective-permute-start(f32[512,256]{1,0:T(8,128)S(1)} %get-tuple-element.18), channel_id=1, source_target_pairs={{64,0},{80,16},{96,32},{112,48},{128,64},{144,80},{160,96},{176,11... | collective-permute-start | bytes 1572872 | tf_op jit(solution)/shard_map/ppermute | solution.py:14
  341.8 21.5 %collective-permute-start.18 = (f32[512,256]{1,0:T(8,128)S(1)}, f32[512,256]{1,0:T(8,128)S(1)}, u32[]{:S(2)}, u32[]{:S(2)}) collective-permute-start(f32[512,256]{1,0:T(8,128)S(1)} %get-tuple-element.5), channel_id=1, source_target_pairs={{0,16},{16,32},{32,48},{48,64},{64,80},{80,96},{96,112},{112,128},... | collective-permute-start | bytes 1572872 | tf_op jit(solution)/shard_map/ppermute | solution.py:14
  345.3 57.6 %collective-permute-start.23 = (f32[512,256]{1,0:T(8,128)}, f32[512,256]{1,0:T(8,128)}, u32[]{:S(2)}, u32[]{:S(2)}) collective-permute-start(f32[512,256]{1,0:T(8,128)} %get-tuple-element.6), channel_id=1, source_target_pairs={{0,96},{16,112},{32,128},{48,144},{64,160},{80,176},{96,192},{112,... | collective-permute-start | bytes 1572872 | tf_op jit(solution)/shard_map/ppermute | solution.py:14
  348.1 79.1 %collective-permute-start.22 = (f32[512,256]{1,0:T(8,128)}, f32[512,256]{1,0:T(8,128)}, u32[]{:S(2)}, u32[]{:S(2)}) collective-permute-start(f32[512,256]{1,0:T(8,128)} %get-tuple-element.7), channel_id=1, source_target_pairs={{0,80},{16,96},{32,112},{48,128},{64,144},{80,160},{96,176},{112,1... | collective-permute-start | bytes 1572872 | tf_op jit(solution)/shard_map/ppermute | solution.py:14
  350.0 95.4 %collective-permute-start.21 = (f32[512,256]{1,0:T(8,128)}, f32[512,256]{1,0:T(8,128)}, u32[]{:S(2)}, u32[]{:S(2)}) collective-permute-start(f32[512,256]{1,0:T(8,128)} %get-tuple-element.8), channel_id=1, source_target_pairs={{0,64},{16,80},{32,96},{48,112},{64,128},{80,144},{96,160},{112,17... | collective-permute-start | bytes 1572872 | tf_op jit(solution)/shard_map/ppermute | solution.py:14
  361.3 90.3 %collective-permute-start.20 = (f32[512,256]{1,0:T(8,128)}, f32[512,256]{1,0:T(8,128)}, u32[]{:S(2)}, u32[]{:S(2)}) collective-permute-start(f32[512,256]{1,0:T(8,128)} %get-tuple-element.9), channel_id=1, source_target_pairs={{0,48},{16,64},{32,80},{48,96},{64,112},{80,128},{96,144},{112,160... | collective-permute-start | bytes 1572872 | tf_op jit(solution)/shard_map/ppermute | solution.py:14
  363.2 7.9 %copy-start.6 = (f32[512,256]{1,0:T(8,128)}, f32[512,256]{1,0:T(8,128)S(1)}, u32[]{:S(2)}) copy-start(f32[512,256]{1,0:T(8,128)S(1)} %collective-permute-done.18) | copy-start | bytes 1572868
  363.2 102.0 %collective-permute-start.19 = (f32[512,256]{1,0:T(8,128)S(1)}, f32[512,256]{1,0:T(8,128)}, u32[]{:S(2)}, u32[]{:S(2)}) collective-permute-start(f32[512,256]{1,0:T(8,128)S(1)} %get-tuple-element.10), channel_id=1, source_target_pairs={{0,32},{16,48},{32,64},{48,80},{64,96},{80,112},{96,128},{112,144}... | collective-permute-start | bytes 1572872 | tf_op jit(solution)/shard_map/ppermute | solution.py:14
Sparse Core Ops, SparseCore 0:
  19.6 77.3 all-gather.4
  249.6 75.2 all-gather.6
